TPU v7x, 128 devices: a whole 4x4x4 slice. The times are simulated.
128 devices in a mesh: ctx: 64 (over x, y, z_lo, core), head: 2 (over z_hi).
Axes of the slice: x: 4, y: 4, z: 4 (z_hi: 2, z_lo: 2; z = z_hi * 2 + z_lo), core: 2. Of those that a mesh axis runs over, the one named last changes fastest.
Arguments:
- queries: bfloat16 [8, 64, 128], P('head', 'ctx'), may hold values from -192 to 192
- incoming_keys: bfloat16 [8, 8, 128], P('head'), may hold values from -6 to 6
- incoming_values: bfloat16 [8, 8, 128], P('head'), may hold values from -6 to 6
- paged_cache: bfloat16 [768, 2, 256, 1024], P('ctx', None, None, 'head'), may hold values from -6 to 6
- page_table: int32 [4, 192], replicated, may hold values from 0 to 767, as said below
- lengths: int32 [4], replicated, may hold values from 1 to 49152, as said below
Outputs:
- attended: bfloat16 [8, 64, 128], P('head', 'ctx')
Inputs may be any that keep to these rules, and one draw needn't show every extreme that they name: `page_table`: a permutation of the 768 global slots: every slot holds exactly one page. `lengths`: some sequence has exactly 49152 cached tokens.
All inputs are finite; a program needn't handle non-finite values.
Results may differ from a plain program's by a relative error of at most 0.0118.
Values may be sent and summed in bfloat16 or wider, within the bound.
A program may use at most 64 MiB of HBM per device.

v0:
```python
import jax
import jax.numpy as jnp
from jax import lax
from jax.sharding import PartitionSpec as P

QUERY_HEADS = 64
KEY_VALUE_HEADS = 8
HEAD_SIZE = 128
NEW_TOKENS = 2


NEG = -1e30


def from_behind(block, axis, distance):
    devices = range(lax.axis_size(axis))
    route = [((i - distance) % len(devices), i) for i in devices]
    return lax.ppermute(block, axis, route)


def combine(first, second):
    top = jnp.maximum(first[0], second[0])
    left = jnp.exp(first[0] - top)
    right = jnp.exp(second[0] - top)
    total = left * first[1] + right * second[1]
    mixed = left[..., None] * first[2] + right[..., None] * second[2]
    return (top, total, mixed)


def on_device(queries, incoming_keys, incoming_values, paged_cache, page_table, lengths):
    slots = paged_cache.shape[0]
    page = paged_cache.shape[2]
    kv_local = queries.shape[0]
    row_count = queries.shape[1]
    query_group = QUERY_HEADS // KEY_VALUE_HEADS
    seq_rows = NEW_TOKENS * query_group
    scale = HEAD_SIZE ** (-0.5)
    cycle_size = lax.axis_size("ctx")
    my_index = lax.axis_index("ctx")
    seq_count = page_table.shape[0]
    slot_ids = my_index * slots + jnp.arange(slots, dtype=jnp.int32)
    match = (page_table[:, :, None] == slot_ids[None, None, :]).astype(jnp.int32)
    slot_seq = jnp.sum(match * jnp.arange(seq_count, dtype=jnp.int32)[:, None, None], axis=(0, 1))
    slot_page = jnp.sum(
        match * jnp.arange(page_table.shape[1], dtype=jnp.int32)[None, :, None], axis=(0, 1)
    )
    owner = slot_seq[None, :] == jnp.arange(seq_count, dtype=jnp.int32)[:, None]
    slot_len = jnp.sum(jnp.where(owner, lengths[:, None], 0), axis=0)
    position = slot_page[:, None] * page + jnp.arange(page, dtype=jnp.int32)[None, :]
    valid = position < slot_len[:, None]
    page_keys = paged_cache[:, 0].reshape(slots, page, kv_local, HEAD_SIZE)
    page_values = paged_cache[:, 1].reshape(slots, page, kv_local, HEAD_SIZE)
    local_rows = jnp.arange(row_count, dtype=jnp.int32)
    flat_keys = page_keys.reshape(slots * page, kv_local, HEAD_SIZE)
    flat_values = page_values.reshape(slots * page, kv_local, HEAD_SIZE)
    flat_valid = valid.reshape(slots * page)
    flat_seq = jnp.broadcast_to(slot_seq[:, None], (slots, page)).reshape(slots * page)

    def visit(anchor, block):
        block_seq = (anchor * row_count + local_rows) // seq_rows
        scores = (
            jnp.einsum("hrd,nhd->hrn", block, flat_keys, preferred_element_type=jnp.float32) * scale
        )
        usable = (flat_valid[None, :] & (flat_seq[None, :] == block_seq[:, None]))[None]
        scores = jnp.where(usable, scores, NEG)
        top = jnp.max(scores, axis=-1)
        weights = jnp.where(usable, jnp.exp(scores - top[..., None]), 0.0)
        total = jnp.sum(weights, axis=-1)
        mixed = jnp.einsum(
            "hrn,nhd->hrd",
            weights.astype(jnp.bfloat16),
            flat_values,
            preferred_element_type=jnp.float32,
        )
        return (top, total, mixed)

    def turn(step, carry):
        block, top, total, mixed = carry
        anchor = (my_index - step) % cycle_size
        top, total, mixed = combine((top, total, mixed), visit(anchor, block))
        block = from_behind(block, "ctx", 1)
        top, total, mixed = from_behind((top, total, mixed), "ctx", 1)
        return (block, top, total, mixed)

    start = (
        queries,
        jnp.full((kv_local, row_count), NEG, jnp.float32),
        jnp.zeros((kv_local, row_count), jnp.float32),
        jnp.zeros((kv_local, row_count, HEAD_SIZE), jnp.float32),
    )
    finished = lax.fori_loop(0, cycle_size, turn, start)
    gathered_part = (finished[1], finished[2], finished[3])
    own_rows = my_index * row_count + local_rows
    row_seq = own_rows // seq_rows
    row_step = own_rows % seq_rows // query_group
    fresh_keys = jnp.take(
        incoming_keys.reshape(kv_local, seq_count, NEW_TOKENS, HEAD_SIZE), row_seq, axis=1
    )
    fresh_values = jnp.take(
        incoming_values.reshape(kv_local, seq_count, NEW_TOKENS, HEAD_SIZE), row_seq, axis=1
    )
    fresh = (
        jnp.einsum("hrd,hrud->hru", queries, fresh_keys, preferred_element_type=jnp.float32) * scale
    )
    fresh_mask = (jnp.arange(NEW_TOKENS, dtype=jnp.int32)[None, :] <= row_step[:, None])[None]
    fresh = jnp.where(fresh_mask, fresh, NEG)
    fresh_top = jnp.max(fresh, axis=-1)
    fresh_w = jnp.where(fresh_mask, jnp.exp(fresh - fresh_top[..., None]), 0.0)
    fresh_total = jnp.sum(fresh_w, axis=-1)
    fresh_mixed = jnp.einsum(
        "hru,hrud->hrd",
        fresh_w.astype(jnp.bfloat16),
        fresh_values,
        preferred_element_type=jnp.float32,
    )
    top, total, mixed = combine(gathered_part, (fresh_top, fresh_total, fresh_mixed))
    return (mixed / total[..., None]).astype(jnp.bfloat16)


def solution(mesh):
    in_specs = (
        P("head", "ctx", None),
        P("head", None, None),
        P("head", None, None),
        P("ctx", None, None, "head"),
        P(),
        P(),
    )
    out_specs = P("head", "ctx", None)
    return jax.shard_map(
        on_device, mesh=mesh, in_specs=in_specs, out_specs=out_specs, check_vma=False
    )
```

profile of v0, /device:TPU:1, one launch (start us, length us, event | category | flops | bytes accessed | tf_op | source)
XLA Modules:
  0.0 672.6 jit_solution(17304116883623371135)
XLA Ops:
  19.2 651.9 %while.23 = (s32[]{:T(128)}, bf16[4,1,128]{2,0,1:T(4,128)(2,1)S(1)}, f32[4,1]{0,1:T(1,128)S(1)}, f32[4,1]{0,1:T(1,128)S(1)}, f32[4,1,128]{2,1,0:T(1,128)S(1)}, /...) while((s32[]{:T(128)}, ...), condition=%wide.region_6.7_spmd.clone, body=%wide.region_3.6_spmd.clone.sunk | while | flops 6412857 | bytes 19115132 | solution.py:91
  59.8 7.2 %collective-permute-done.1 = f32[4,1]{0,1:T(1,128)S(1)} collective-permute-done((f32[4,1]{0,1:T(1,128)S(1)}, f32[4,1]{0,1:T(1,128)S(1)}, u32[]{:S(2)}, u32[]{:S(2)}) %collective-permute-start.1) | collective-permute-done | bytes 48 | tf_op jit(solution)/shard_map/while/body/eval_jaxpr/ppermute | solution.py:18
  70.1 7.2 %collective-permute-done.1 = f32[4,1]{0,1:T(1,128)S(1)} collective-permute-done((f32[4,1]{0,1:T(1,128)S(1)}, f32[4,1]{0,1:T(1,128)S(1)}, u32[]{:S(2)}, u32[]{:S(2)}) %collective-permute-start.1) | collective-permute-done | bytes 48 | tf_op jit(solution)/shard_map/while/body/eval_jaxpr/ppermute | solution.py:18
  80.3 7.2 %collective-permute-done.1 = f32[4,1]{0,1:T(1,128)S(1)} collective-permute-done((f32[4,1]{0,1:T(1,128)S(1)}, f32[4,1]{0,1:T(1,128)S(1)}, u32[]{:S(2)}, u32[]{:S(2)}) %collective-permute-start.1) | collective-permute-done | bytes 48 | tf_op jit(solution)/shard_map/while/body/eval_jaxpr/ppermute | solution.py:18
  90.5 7.2 %collective-permute-done.1 = f32[4,1]{0,1:T(1,128)S(1)} collective-permute-done((f32[4,1]{0,1:T(1,128)S(1)}, f32[4,1]{0,1:T(1,128)S(1)}, u32[]{:S(2)}, u32[]{:S(2)}) %collective-permute-start.1) | collective-permute-done | bytes 48 | tf_op jit(solution)/shard_map/while/body/eval_jaxpr/ppermute | solution.py:18
  100.8 7.2 %collective-permute-done.1 = f32[4,1]{0,1:T(1,128)S(1)} collective-permute-done((f32[4,1]{0,1:T(1,128)S(1)}, f32[4,1]{0,1:T(1,128)S(1)}, u32[]{:S(2)}, u32[]{:S(2)}) %collective-permute-start.1) | collective-permute-done | bytes 48 | tf_op jit(solution)/shard_map/while/body/eval_jaxpr/ppermute | solution.py:18
  111.0 7.2 %collective-permute-done.1 = f32[4,1]{0,1:T(1,128)S(1)} collective-permute-done((f32[4,1]{0,1:T(1,128)S(1)}, f32[4,1]{0,1:T(1,128)S(1)}, u32[]{:S(2)}, u32[]{:S(2)}) %collective-permute-start.1) | collective-permute-done | bytes 48 | tf_op jit(solution)/shard_map/while/body/eval_jaxpr/ppermute | solution.py:18
  121.3 7.2 %collective-permute-done.1 = f32[4,1]{0,1:T(1,128)S(1)} collective-permute-done((f32[4,1]{0,1:T(1,128)S(1)}, f32[4,1]{0,1:T(1,128)S(1)}, u32[]{:S(2)}, u32[]{:S(2)}) %collective-permute-start.1) | collective-permute-done | bytes 48 | tf_op jit(solution)/shard_map/while/body/eval_jaxpr/ppermute | solution.py:18
  131.5 7.2 %collective-permute-done.1 = f32[4,1]{0,1:T(1,128)S(1)} collective-permute-done((f32[4,1]{0,1:T(1,128)S(1)}, f32[4,1]{0,1:T(1,128)S(1)}, u32[]{:S(2)}, u32[]{:S(2)}) %collective-permute-start.1) | collective-permute-done | bytes 48 | tf_op jit(solution)/shard_map/while/body/eval_jaxpr/ppermute | solution.py:18
  141.7 7.2 %collective-permute-done.1 = f32[4,1]{0,1:T(1,128)S(1)} collective-permute-done((f32[4,1]{0,1:T(1,128)S(1)}, f32[4,1]{0,1:T(1,128)S(1)}, u32[]{:S(2)}, u32[]{:S(2)}) %collective-permute-start.1) | collective-permute-done | bytes 48 | tf_op jit(solution)/shard_map/while/body/eval_jaxpr/ppermute | solution.py:18
  152.0 7.2 %collective-permute-done.1 = f32[4,1]{0,1:T(1,128)S(1)} collective-permute-done((f32[4,1]{0,1:T(1,128)S(1)}, f32[4,1]{0,1:T(1,128)S(1)}, u32[]{:S(2)}, u32[]{:S(2)}) %collective-permute-start.1) | collective-permute-done | bytes 48 | tf_op jit(solution)/shard_map/while/body/eval_jaxpr/ppermute | solution.py:18
  162.2 7.2 %collective-permute-done.1 = f32[4,1]{0,1:T(1,128)S(1)} collective-permute-done((f32[4,1]{0,1:T(1,128)S(1)}, f32[4,1]{0,1:T(1,128)S(1)}, u32[]{:S(2)}, u32[]{:S(2)}) %collective-permute-start.1) | collective-permute-done | bytes 48 | tf_op jit(solution)/shard_map/while/body/eval_jaxpr/ppermute | solution.py:18
  172.4 7.2 %collective-permute-done.1 = f32[4,1]{0,1:T(1,128)S(1)} collective-permute-done((f32[4,1]{0,1:T(1,128)S(1)}, f32[4,1]{0,1:T(1,128)S(1)}, u32[]{:S(2)}, u32[]{:S(2)}) %collective-permute-start.1) | collective-permute-done | bytes 48 | tf_op jit(solution)/shard_map/while/body/eval_jaxpr/ppermute | solution.py:18
  182.7 7.2 %collective-permute-done.1 = f32[4,1]{0,1:T(1,128)S(1)} collective-permute-done((f32[4,1]{0,1:T(1,128)S(1)}, f32[4,1]{0,1:T(1,128)S(1)}, u32[]{:S(2)}, u32[]{:S(2)}) %collective-permute-start.1) | collective-permute-done | bytes 48 | tf_op jit(solution)/shard_map/while/body/eval_jaxpr/ppermute | solution.py:18
  192.9 7.2 %collective-permute-done.1 = f32[4,1]{0,1:T(1,128)S(1)} collective-permute-done((f32[4,1]{0,1:T(1,128)S(1)}, f32[4,1]{0,1:T(1,128)S(1)}, u32[]{:S(2)}, u32[]{:S(2)}) %collective-permute-start.1) | collective-permute-done | bytes 48 | tf_op jit(solution)/shard_map/while/body/eval_jaxpr/ppermute | solution.py:18
  203.1 7.2 %collective-permute-done.1 = f32[4,1]{0,1:T(1,128)S(1)} collective-permute-done((f32[4,1]{0,1:T(1,128)S(1)}, f32[4,1]{0,1:T(1,128)S(1)}, u32[]{:S(2)}, u32[]{:S(2)}) %collective-permute-start.1) | collective-permute-done | bytes 48 | tf_op jit(solution)/shard_map/while/body/eval_jaxpr/ppermute | solution.py:18
  213.4 7.2 %collective-permute-done.1 = f32[4,1]{0,1:T(1,128)S(1)} collective-permute-done((f32[4,1]{0,1:T(1,128)S(1)}, f32[4,1]{0,1:T(1,128)S(1)}, u32[]{:S(2)}, u32[]{:S(2)}) %collective-permute-start.1) | collective-permute-done | bytes 48 | tf_op jit(solution)/shard_map/while/body/eval_jaxpr/ppermute | solution.py:18
  223.6 7.2 %collective-permute-done.1 = f32[4,1]{0,1:T(1,128)S(1)} collective-permute-done((f32[4,1]{0,1:T(1,128)S(1)}, f32[4,1]{0,1:T(1,128)S(1)}, u32[]{:S(2)}, u32[]{:S(2)}) %collective-permute-start.1) | collective-permute-done | bytes 48 | tf_op jit(solution)/shard_map/while/body/eval_jaxpr/ppermute | solution.py:18
  233.9 7.2 %collective-permute-done.1 = f32[4,1]{0,1:T(1,128)S(1)} collective-permute-done((f32[4,1]{0,1:T(1,128)S(1)}, f32[4,1]{0,1:T(1,128)S(1)}, u32[]{:S(2)}, u32[]{:S(2)}) %collective-permute-start.1) | collective-permute-done | bytes 48 | tf_op jit(solution)/shard_map/while/body/eval_jaxpr/ppermute | solution.py:18
  244.1 7.2 %collective-permute-done.1 = f32[4,1]{0,1:T(1,128)S(1)} collective-permute-done((f32[4,1]{0,1:T(1,128)S(1)}, f32[4,1]{0,1:T(1,128)S(1)}, u32[]{:S(2)}, u32[]{:S(2)}) %collective-permute-start.1) | collective-permute-done | bytes 48 | tf_op jit(solution)/shard_map/while/body/eval_jaxpr/ppermute | solution.py:18
  254.3 7.2 %collective-permute-done.1 = f32[4,1]{0,1:T(1,128)S(1)} collective-permute-done((f32[4,1]{0,1:T(1,128)S(1)}, f32[4,1]{0,1:T(1,128)S(1)}, u32[]{:S(2)}, u32[]{:S(2)}) %collective-permute-start.1) | collective-permute-done | bytes 48 | tf_op jit(solution)/shard_map/while/body/eval_jaxpr/ppermute | solution.py:18
  264.6 7.2 %collective-permute-done.1 = f32[4,1]{0,1:T(1,128)S(1)} collective-permute-done((f32[4,1]{0,1:T(1,128)S(1)}, f32[4,1]{0,1:T(1,128)S(1)}, u32[]{:S(2)}, u32[]{:S(2)}) %collective-permute-start.1) | collective-permute-done | bytes 48 | tf_op jit(solution)/shard_map/while/body/eval_jaxpr/ppermute | solution.py:18
  274.8 7.2 %collective-permute-done.1 = f32[4,1]{0,1:T(1,128)S(1)} collective-permute-done((f32[4,1]{0,1:T(1,128)S(1)}, f32[4,1]{0,1:T(1,128)S(1)}, u32[]{:S(2)}, u32[]{:S(2)}) %collective-permute-start.1) | collective-permute-done | bytes 48 | tf_op jit(solution)/shard_map/while/body/eval_jaxpr/ppermute | solution.py:18
  285.0 7.2 %collective-permute-done.1 = f32[4,1]{0,1:T(1,128)S(1)} collective-permute-done((f32[4,1]{0,1:T(1,128)S(1)}, f32[4,1]{0,1:T(1,128)S(1)}, u32[]{:S(2)}, u32[]{:S(2)}) %collective-permute-start.1) | collective-permute-done | bytes 48 | tf_op jit(solution)/shard_map/while/body/eval_jaxpr/ppermute | solution.py:18
  295.3 7.2 %collective-permute-done.1 = f32[4,1]{0,1:T(1,128)S(1)} collective-permute-done((f32[4,1]{0,1:T(1,128)S(1)}, f32[4,1]{0,1:T(1,128)S(1)}, u32[]{:S(2)}, u32[]{:S(2)}) %collective-permute-start.1) | collective-permute-done | bytes 48 | tf_op jit(solution)/shard_map/while/body/eval_jaxpr/ppermute | solution.py:18
  305.5 7.2 %collective-permute-done.1 = f32[4,1]{0,1:T(1,128)S(1)} collective-permute-done((f32[4,1]{0,1:T(1,128)S(1)}, f32[4,1]{0,1:T(1,128)S(1)}, u32[]{:S(2)}, u32[]{:S(2)}) %collective-permute-start.1) | collective-permute-done | bytes 48 | tf_op jit(solution)/shard_map/while/body/eval_jaxpr/ppermute | solution.py:18
  315.7 7.2 %collective-permute-done.1 = f32[4,1]{0,1:T(1,128)S(1)} collective-permute-done((f32[4,1]{0,1:T(1,128)S(1)}, f32[4,1]{0,1:T(1,128)S(1)}, u32[]{:S(2)}, u32[]{:S(2)}) %collective-permute-start.1) | collective-permute-done | bytes 48 | tf_op jit(solution)/shard_map/while/body/eval_jaxpr/ppermute | solution.py:18
  326.0 7.2 %collective-permute-done.1 = f32[4,1]{0,1:T(1,128)S(1)} collective-permute-done((f32[4,1]{0,1:T(1,128)S(1)}, f32[4,1]{0,1:T(1,128)S(1)}, u32[]{:S(2)}, u32[]{:S(2)}) %collective-permute-start.1) | collective-permute-done | bytes 48 | tf_op jit(solution)/shard_map/while/body/eval_jaxpr/ppermute | solution.py:18
  336.2 7.2 %collective-permute-done.1 = f32[4,1]{0,1:T(1,128)S(1)} collective-permute-done((f32[4,1]{0,1:T(1,128)S(1)}, f32[4,1]{0,1:T(1,128)S(1)}, u32[]{:S(2)}, u32[]{:S(2)}) %collective-permute-start.1) | collective-permute-done | bytes 48 | tf_op jit(solution)/shard_map/while/body/eval_jaxpr/ppermute | solution.py:18
  346.5 7.2 %collective-permute-done.1 = f32[4,1]{0,1:T(1,128)S(1)} collective-permute-done((f32[4,1]{0,1:T(1,128)S(1)}, f32[4,1]{0,1:T(1,128)S(1)}, u32[]{:S(2)}, u32[]{:S(2)}) %collective-permute-start.1) | collective-permute-done | bytes 48 | tf_op jit(solution)/shard_map/while/body/eval_jaxpr/ppermute | solution.py:18
  356.7 7.2 %collective-permute-done.1 = f32[4,1]{0,1:T(1,128)S(1)} collective-permute-done((f32[4,1]{0,1:T(1,128)S(1)}, f32[4,1]{0,1:T(1,128)S(1)}, u32[]{:S(2)}, u32[]{:S(2)}) %collective-permute-start.1) | collective-permute-done | bytes 48 | tf_op jit(solution)/shard_map/while/body/eval_jaxpr/ppermute | solution.py:18
  366.9 7.2 %collective-permute-done.1 = f32[4,1]{0,1:T(1,128)S(1)} collective-permute-done((f32[4,1]{0,1:T(1,128)S(1)}, f32[4,1]{0,1:T(1,128)S(1)}, u32[]{:S(2)}, u32[]{:S(2)}) %collective-permute-start.1) | collective-permute-done | bytes 48 | tf_op jit(solution)/shard_map/while/body/eval_jaxpr/ppermute | solution.py:18
  377.2 7.2 %collective-permute-done.1 = f32[4,1]{0,1:T(1,128)S(1)} collective-permute-done((f32[4,1]{0,1:T(1,128)S(1)}, f32[4,1]{0,1:T(1,128)S(1)}, u32[]{:S(2)}, u32[]{:S(2)}) %collective-permute-start.1) | collective-permute-done | bytes 48 | tf_op jit(solution)/shard_map/while/body/eval_jaxpr/ppermute | solution.py:18
  387.4 7.2 %collective-permute-done.1 = f32[4,1]{0,1:T(1,128)S(1)} collective-permute-done((f32[4,1]{0,1:T(1,128)S(1)}, f32[4,1]{0,1:T(1,128)S(1)}, u32[]{:S(2)}, u32[]{:S(2)}) %collective-permute-start.1) | collective-permute-done | bytes 48 | tf_op jit(solution)/shard_map/while/body/eval_jaxpr/ppermute | solution.py:18
  397.6 7.2 %collective-permute-done.1 = f32[4,1]{0,1:T(1,128)S(1)} collective-permute-done((f32[4,1]{0,1:T(1,128)S(1)}, f32[4,1]{0,1:T(1,128)S(1)}, u32[]{:S(2)}, u32[]{:S(2)}) %collective-permute-start.1) | collective-permute-done | bytes 48 | tf_op jit(solution)/shard_map/while/body/eval_jaxpr/ppermute | solution.py:18
  407.9 7.2 %collective-permute-done.1 = f32[4,1]{0,1:T(1,128)S(1)} collective-permute-done((f32[4,1]{0,1:T(1,128)S(1)}, f32[4,1]{0,1:T(1,128)S(1)}, u32[]{:S(2)}, u32[]{:S(2)}) %collective-permute-start.1) | collective-permute-done | bytes 48 | tf_op jit(solution)/shard_map/while/body/eval_jaxpr/ppermute | solution.py:18
  418.1 7.2 %collective-permute-done.1 = f32[4,1]{0,1:T(1,128)S(1)} collective-permute-done((f32[4,1]{0,1:T(1,128)S(1)}, f32[4,1]{0,1:T(1,128)S(1)}, u32[]{:S(2)}, u32[]{:S(2)}) %collective-permute-start.1) | collective-permute-done | bytes 48 | tf_op jit(solution)/shard_map/while/body/eval_jaxpr/ppermute | solution.py:18
  428.3 7.2 %collective-permute-done.1 = f32[4,1]{0,1:T(1,128)S(1)} collective-permute-done((f32[4,1]{0,1:T(1,128)S(1)}, f32[4,1]{0,1:T(1,128)S(1)}, u32[]{:S(2)}, u32[]{:S(2)}) %collective-permute-start.1) | collective-permute-done | bytes 48 | tf_op jit(solution)/shard_map/while/body/eval_jaxpr/ppermute | solution.py:18
  438.6 7.2 %collective-permute-done.1 = f32[4,1]{0,1:T(1,128)S(1)} collective-permute-done((f32[4,1]{0,1:T(1,128)S(1)}, f32[4,1]{0,1:T(1,128)S(1)}, u32[]{:S(2)}, u32[]{:S(2)}) %collective-permute-start.1) | collective-permute-done | bytes 48 | tf_op jit(solution)/shard_map/while/body/eval_jaxpr/ppermute | solution.py:18
  448.8 7.2 %collective-permute-done.1 = f32[4,1]{0,1:T(1,128)S(1)} collective-permute-done((f32[4,1]{0,1:T(1,128)S(1)}, f32[4,1]{0,1:T(1,128)S(1)}, u32[]{:S(2)}, u32[]{:S(2)}) %collective-permute-start.1) | collective-permute-done | bytes 48 | tf_op jit(solution)/shard_map/while/body/eval_jaxpr/ppermute | solution.py:18
  479.5 7.2 %collective-permute-done.1 = f32[4,1]{0,1:T(1,128)S(1)} collective-permute-done((f32[4,1]{0,1:T(1,128)S(1)}, f32[4,1]{0,1:T(1,128)S(1)}, u32[]{:S(2)}, u32[]{:S(2)}) %collective-permute-start.1) | collective-permute-done | bytes 48 | tf_op jit(solution)/shard_map/while/body/eval_jaxpr/ppermute | solution.py:18
  489.8 7.2 %collective-permute-done.1 = f32[4,1]{0,1:T(1,128)S(1)} collective-permute-done((f32[4,1]{0,1:T(1,128)S(1)}, f32[4,1]{0,1:T(1,128)S(1)}, u32[]{:S(2)}, u32[]{:S(2)}) %collective-permute-start.1) | collective-permute-done | bytes 48 | tf_op jit(solution)/shard_map/while/body/eval_jaxpr/ppermute | solution.py:18
  530.7 7.2 %collective-permute-done.1 = f32[4,1]{0,1:T(1,128)S(1)} collective-permute-done((f32[4,1]{0,1:T(1,128)S(1)}, f32[4,1]{0,1:T(1,128)S(1)}, u32[]{:S(2)}, u32[]{:S(2)}) %collective-permute-start.1) | collective-permute-done | bytes 48 | tf_op jit(solution)/shard_map/while/body/eval_jaxpr/ppermute | solution.py:18
  540.9 7.2 %collective-permute-done.1 = f32[4,1]{0,1:T(1,128)S(1)} collective-permute-done((f32[4,1]{0,1:T(1,128)S(1)}, f32[4,1]{0,1:T(1,128)S(1)}, u32[]{:S(2)}, u32[]{:S(2)}) %collective-permute-start.1) | collective-permute-done | bytes 48 | tf_op jit(solution)/shard_map/while/body/eval_jaxpr/ppermute | solution.py:18
  581.9 7.2 %collective-permute-done.1 = f32[4,1]{0,1:T(1,128)S(1)} collective-permute-done((f32[4,1]{0,1:T(1,128)S(1)}, f32[4,1]{0,1:T(1,128)S(1)}, u32[]{:S(2)}, u32[]{:S(2)}) %collective-permute-start.1) | collective-permute-done | bytes 48 | tf_op jit(solution)/shard_map/while/body/eval_jaxpr/ppermute | solution.py:18
  592.1 7.2 %collective-permute-done.1 = f32[4,1]{0,1:T(1,128)S(1)} collective-permute-done((f32[4,1]{0,1:T(1,128)S(1)}, f32[4,1]{0,1:T(1,128)S(1)}, u32[]{:S(2)}, u32[]{:S(2)}) %collective-permute-start.1) | collective-permute-done | bytes 48 | tf_op jit(solution)/shard_map/while/body/eval_jaxpr/ppermute | solution.py:18
  633.1 7.2 %collective-permute-done.1 = f32[4,1]{0,1:T(1,128)S(1)} collective-permute-done((f32[4,1]{0,1:T(1,128)S(1)}, f32[4,1]{0,1:T(1,128)S(1)}, u32[]{:S(2)}, u32[]{:S(2)}) %collective-permute-start.1) | collective-permute-done | bytes 48 | tf_op jit(solution)/shard_map/while/body/eval_jaxpr/ppermute | solution.py:18
  643.3 7.2 %collective-permute-done.1 = f32[4,1]{0,1:T(1,128)S(1)} collective-permute-done((f32[4,1]{0,1:T(1,128)S(1)}, f32[4,1]{0,1:T(1,128)S(1)}, u32[]{:S(2)}, u32[]{:S(2)}) %collective-permute-start.1) | collective-permute-done | bytes 48 | tf_op jit(solution)/shard_map/while/body/eval_jaxpr/ppermute | solution.py:18
  (1317 shorter events, 330.3 us)
Async XLA Ops:
  39.1 7.5 %collective-permute-start.3 = (f32[4,1,128]{2,1,0:T(1,128)S(1)}, f32[4,1,128]{2,1,0:T(1,128)S(1)}, u32[]{:S(2)}, u32[]{:S(2)}) collective-permute-start(f32[4,1,128]{2,1,0:T(1,128)S(1)} %multiply_add_fusion.2), channel_id=1, source_target_pairs={{126,0},{0,2},{2,4},{4,6},{6,8},{8,10},{10,12},{12,14},{14,16},{16... | collective-permute-start | bytes 6152 | tf_op jit(solution)/shard_map/while/body/eval_jaxpr/ppermute | solution.py:18
  49.4 7.5 %collective-permute-start.3 = (f32[4,1,128]{2,1,0:T(1,128)S(1)}, f32[4,1,128]{2,1,0:T(1,128)S(1)}, u32[]{:S(2)}, u32[]{:S(2)}) collective-permute-start(f32[4,1,128]{2,1,0:T(1,128)S(1)} %multiply_add_fusion.2), channel_id=1, source_target_pairs={{126,0},{0,2},{2,4},{4,6},{6,8},{8,10},{10,12},{12,14},{14,16},{16... | collective-permute-start | bytes 6152 | tf_op jit(solution)/shard_map/while/body/eval_jaxpr/ppermute | solution.py:18
  59.6 7.5 %collective-permute-start.3 = (f32[4,1,128]{2,1,0:T(1,128)S(1)}, f32[4,1,128]{2,1,0:T(1,128)S(1)}, u32[]{:S(2)}, u32[]{:S(2)}) collective-permute-start(f32[4,1,128]{2,1,0:T(1,128)S(1)} %multiply_add_fusion.2), channel_id=1, source_target_pairs={{126,0},{0,2},{2,4},{4,6},{6,8},{8,10},{10,12},{12,14},{14,16},{16... | collective-permute-start | bytes 6152 | tf_op jit(solution)/shard_map/while/body/eval_jaxpr/ppermute | solution.py:18
  69.8 7.5 %collective-permute-start.3 = (f32[4,1,128]{2,1,0:T(1,128)S(1)}, f32[4,1,128]{2,1,0:T(1,128)S(1)}, u32[]{:S(2)}, u32[]{:S(2)}) collective-permute-start(f32[4,1,128]{2,1,0:T(1,128)S(1)} %multiply_add_fusion.2), channel_id=1, source_target_pairs={{126,0},{0,2},{2,4},{4,6},{6,8},{8,10},{10,12},{12,14},{14,16},{16... | collective-permute-start | bytes 6152 | tf_op jit(solution)/shard_map/while/body/eval_jaxpr/ppermute | solution.py:18
  80.1 7.5 %collective-permute-start.3 = (f32[4,1,128]{2,1,0:T(1,128)S(1)}, f32[4,1,128]{2,1,0:T(1,128)S(1)}, u32[]{:S(2)}, u32[]{:S(2)}) collective-permute-start(f32[4,1,128]{2,1,0:T(1,128)S(1)} %multiply_add_fusion.2), channel_id=1, source_target_pairs={{126,0},{0,2},{2,4},{4,6},{6,8},{8,10},{10,12},{12,14},{14,16},{16... | collective-permute-start | bytes 6152 | tf_op jit(solution)/shard_map/while/body/eval_jaxpr/ppermute | solution.py:18
  90.3 7.5 %collective-permute-start.3 = (f32[4,1,128]{2,1,0:T(1,128)S(1)}, f32[4,1,128]{2,1,0:T(1,128)S(1)}, u32[]{:S(2)}, u32[]{:S(2)}) collective-permute-start(f32[4,1,128]{2,1,0:T(1,128)S(1)} %multiply_add_fusion.2), channel_id=1, source_target_pairs={{126,0},{0,2},{2,4},{4,6},{6,8},{8,10},{10,12},{12,14},{14,16},{16... | collective-permute-start | bytes 6152 | tf_op jit(solution)/shard_map/while/body/eval_jaxpr/ppermute | solution.py:18
  100.5 7.5 %collective-permute-start.3 = (f32[4,1,128]{2,1,0:T(1,128)S(1)}, f32[4,1,128]{2,1,0:T(1,128)S(1)}, u32[]{:S(2)}, u32[]{:S(2)}) collective-permute-start(f32[4,1,128]{2,1,0:T(1,128)S(1)} %multiply_add_fusion.2), channel_id=1, source_target_pairs={{126,0},{0,2},{2,4},{4,6},{6,8},{8,10},{10,12},{12,14},{14,16},{16... | collective-permute-start | bytes 6152 | tf_op jit(solution)/shard_map/while/body/eval_jaxpr/ppermute | solution.py:18
  110.8 7.5 %collective-permute-start.3 = (f32[4,1,128]{2,1,0:T(1,128)S(1)}, f32[4,1,128]{2,1,0:T(1,128)S(1)}, u32[]{:S(2)}, u32[]{:S(2)}) collective-permute-start(f32[4,1,128]{2,1,0:T(1,128)S(1)} %multiply_add_fusion.2), channel_id=1, source_target_pairs={{126,0},{0,2},{2,4},{4,6},{6,8},{8,10},{10,12},{12,14},{14,16},{16... | collective-permute-start | bytes 6152 | tf_op jit(solution)/shard_map/while/body/eval_jaxpr/ppermute | solution.py:18
  121.0 7.5 %collective-permute-start.3 = (f32[4,1,128]{2,1,0:T(1,128)S(1)}, f32[4,1,128]{2,1,0:T(1,128)S(1)}, u32[]{:S(2)}, u32[]{:S(2)}) collective-permute-start(f32[4,1,128]{2,1,0:T(1,128)S(1)} %multiply_add_fusion.2), channel_id=1, source_target_pairs={{126,0},{0,2},{2,4},{4,6},{6,8},{8,10},{10,12},{12,14},{14,16},{16... | collective-permute-start | bytes 6152 | tf_op jit(solution)/shard_map/while/body/eval_jaxpr/ppermute | solution.py:18
  131.2 7.5 %collective-permute-start.3 = (f32[4,1,128]{2,1,0:T(1,128)S(1)}, f32[4,1,128]{2,1,0:T(1,128)S(1)}, u32[]{:S(2)}, u32[]{:S(2)}) collective-permute-start(f32[4,1,128]{2,1,0:T(1,128)S(1)} %multiply_add_fusion.2), channel_id=1, source_target_pairs={{126,0},{0,2},{2,4},{4,6},{6,8},{8,10},{10,12},{12,14},{14,16},{16... | collective-permute-start | bytes 6152 | tf_op jit(solution)/shard_map/while/body/eval_jaxpr/ppermute | solution.py:18
  141.5 7.5 %collective-permute-start.3 = (f32[4,1,128]{2,1,0:T(1,128)S(1)}, f32[4,1,128]{2,1,0:T(1,128)S(1)}, u32[]{:S(2)}, u32[]{:S(2)}) collective-permute-start(f32[4,1,128]{2,1,0:T(1,128)S(1)} %multiply_add_fusion.2), channel_id=1, source_target_pairs={{126,0},{0,2},{2,4},{4,6},{6,8},{8,10},{10,12},{12,14},{14,16},{16... | collective-permute-start | bytes 6152 | tf_op jit(solution)/shard_map/while/body/eval_jaxpr/ppermute | solution.py:18
  151.7 7.5 %collective-permute-start.3 = (f32[4,1,128]{2,1,0:T(1,128)S(1)}, f32[4,1,128]{2,1,0:T(1,128)S(1)}, u32[]{:S(2)}, u32[]{:S(2)}) collective-permute-start(f32[4,1,128]{2,1,0:T(1,128)S(1)} %multiply_add_fusion.2), channel_id=1, source_target_pairs={{126,0},{0,2},{2,4},{4,6},{6,8},{8,10},{10,12},{12,14},{14,16},{16... | collective-permute-start | bytes 6152 | tf_op jit(solution)/shard_map/while/body/eval_jaxpr/ppermute | solution.py:18
  162.0 7.5 %collective-permute-start.3 = (f32[4,1,128]{2,1,0:T(1,128)S(1)}, f32[4,1,128]{2,1,0:T(1,128)S(1)}, u32[]{:S(2)}, u32[]{:S(2)}) collective-permute-start(f32[4,1,128]{2,1,0:T(1,128)S(1)} %multiply_add_fusion.2), channel_id=1, source_target_pairs={{126,0},{0,2},{2,4},{4,6},{6,8},{8,10},{10,12},{12,14},{14,16},{16... | collective-permute-start | bytes 6152 | tf_op jit(solution)/shard_map/while/body/eval_jaxpr/ppermute | solution.py:18
  172.2 7.5 %collective-permute-start.3 = (f32[4,1,128]{2,1,0:T(1,128)S(1)}, f32[4,1,128]{2,1,0:T(1,128)S(1)}, u32[]{:S(2)}, u32[]{:S(2)}) collective-permute-start(f32[4,1,128]{2,1,0:T(1,128)S(1)} %multiply_add_fusion.2), channel_id=1, source_target_pairs={{126,0},{0,2},{2,4},{4,6},{6,8},{8,10},{10,12},{12,14},{14,16},{16... | collective-permute-start | bytes 6152 | tf_op jit(solution)/shard_map/while/body/eval_jaxpr/ppermute | solution.py:18
  182.4 7.5 %collective-permute-start.3 = (f32[4,1,128]{2,1,0:T(1,128)S(1)}, f32[4,1,128]{2,1,0:T(1,128)S(1)}, u32[]{:S(2)}, u32[]{:S(2)}) collective-permute-start(f32[4,1,128]{2,1,0:T(1,128)S(1)} %multiply_add_fusion.2), channel_id=1, source_target_pairs={{126,0},{0,2},{2,4},{4,6},{6,8},{8,10},{10,12},{12,14},{14,16},{16... | collective-permute-start | bytes 6152 | tf_op jit(solution)/shard_map/while/body/eval_jaxpr/ppermute | solution.py:18
  192.7 7.5 %collective-permute-start.3 = (f32[4,1,128]{2,1,0:T(1,128)S(1)}, f32[4,1,128]{2,1,0:T(1,128)S(1)}, u32[]{:S(2)}, u32[]{:S(2)}) collective-permute-start(f32[4,1,128]{2,1,0:T(1,128)S(1)} %multiply_add_fusion.2), channel_id=1, source_target_pairs={{126,0},{0,2},{2,4},{4,6},{6,8},{8,10},{10,12},{12,14},{14,16},{16... | collective-permute-start | bytes 6152 | tf_op jit(solution)/shard_map/while/body/eval_jaxpr/ppermute | solution.py:18
  202.9 7.5 %collective-permute-start.3 = (f32[4,1,128]{2,1,0:T(1,128)S(1)}, f32[4,1,128]{2,1,0:T(1,128)S(1)}, u32[]{:S(2)}, u32[]{:S(2)}) collective-permute-start(f32[4,1,128]{2,1,0:T(1,128)S(1)} %multiply_add_fusion.2), channel_id=1, source_target_pairs={{126,0},{0,2},{2,4},{4,6},{6,8},{8,10},{10,12},{12,14},{14,16},{16... | collective-permute-start | bytes 6152 | tf_op jit(solution)/shard_map/while/body/eval_jaxpr/ppermute | solution.py:18
  213.1 7.5 %collective-permute-start.3 = (f32[4,1,128]{2,1,0:T(1,128)S(1)}, f32[4,1,128]{2,1,0:T(1,128)S(1)}, u32[]{:S(2)}, u32[]{:S(2)}) collective-permute-start(f32[4,1,128]{2,1,0:T(1,128)S(1)} %multiply_add_fusion.2), channel_id=1, source_target_pairs={{126,0},{0,2},{2,4},{4,6},{6,8},{8,10},{10,12},{12,14},{14,16},{16... | collective-permute-start | bytes 6152 | tf_op jit(solution)/shard_map/while/body/eval_jaxpr/ppermute | solution.py:18
  223.4 7.5 %collective-permute-start.3 = (f32[4,1,128]{2,1,0:T(1,128)S(1)}, f32[4,1,128]{2,1,0:T(1,128)S(1)}, u32[]{:S(2)}, u32[]{:S(2)}) collective-permute-start(f32[4,1,128]{2,1,0:T(1,128)S(1)} %multiply_add_fusion.2), channel_id=1, source_target_pairs={{126,0},{0,2},{2,4},{4,6},{6,8},{8,10},{10,12},{12,14},{14,16},{16... | collective-permute-start | bytes 6152 | tf_op jit(solution)/shard_map/while/body/eval_jaxpr/ppermute | solution.py:18
  233.6 7.5 %collective-permute-start.3 = (f32[4,1,128]{2,1,0:T(1,128)S(1)}, f32[4,1,128]{2,1,0:T(1,128)S(1)}, u32[]{:S(2)}, u32[]{:S(2)}) collective-permute-start(f32[4,1,128]{2,1,0:T(1,128)S(1)} %multiply_add_fusion.2), channel_id=1, source_target_pairs={{126,0},{0,2},{2,4},{4,6},{6,8},{8,10},{10,12},{12,14},{14,16},{16... | collective-permute-start | bytes 6152 | tf_op jit(solution)/shard_map/while/body/eval_jaxpr/ppermute | solution.py:18
  243.8 7.5 %collective-permute-start.3 = (f32[4,1,128]{2,1,0:T(1,128)S(1)}, f32[4,1,128]{2,1,0:T(1,128)S(1)}, u32[]{:S(2)}, u32[]{:S(2)}) collective-permute-start(f32[4,1,128]{2,1,0:T(1,128)S(1)} %multiply_add_fusion.2), channel_id=1, source_target_pairs={{126,0},{0,2},{2,4},{4,6},{6,8},{8,10},{10,12},{12,14},{14,16},{16... | collective-permute-start | bytes 6152 | tf_op jit(solution)/shard_map/while/body/eval_jaxpr/ppermute | solution.py:18
  254.1 7.5 %collective-permute-start.3 = (f32[4,1,128]{2,1,0:T(1,128)S(1)}, f32[4,1,128]{2,1,0:T(1,128)S(1)}, u32[]{:S(2)}, u32[]{:S(2)}) collective-permute-start(f32[4,1,128]{2,1,0:T(1,128)S(1)} %multiply_add_fusion.2), channel_id=1, source_target_pairs={{126,0},{0,2},{2,4},{4,6},{6,8},{8,10},{10,12},{12,14},{14,16},{16... | collective-permute-start | bytes 6152 | tf_op jit(solution)/shard_map/while/body/eval_jaxpr/ppermute | solution.py:18
  264.3 7.5 %collective-permute-start.3 = (f32[4,1,128]{2,1,0:T(1,128)S(1)}, f32[4,1,128]{2,1,0:T(1,128)S(1)}, u32[]{:S(2)}, u32[]{:S(2)}) collective-permute-start(f32[4,1,128]{2,1,0:T(1,128)S(1)} %multiply_add_fusion.2), channel_id=1, source_target_pairs={{126,0},{0,2},{2,4},{4,6},{6,8},{8,10},{10,12},{12,14},{14,16},{16... | collective-permute-start | bytes 6152 | tf_op jit(solution)/shard_map/while/body/eval_jaxpr/ppermute | solution.py:18
  274.6 7.5 %collective-permute-start.3 = (f32[4,1,128]{2,1,0:T(1,128)S(1)}, f32[4,1,128]{2,1,0:T(1,128)S(1)}, u32[]{:S(2)}, u32[]{:S(2)}) collective-permute-start(f32[4,1,128]{2,1,0:T(1,128)S(1)} %multiply_add_fusion.2), channel_id=1, source_target_pairs={{126,0},{0,2},{2,4},{4,6},{6,8},{8,10},{10,12},{12,14},{14,16},{16... | collective-permute-start | bytes 6152 | tf_op jit(solution)/shard_map/while/body/eval_jaxpr/ppermute | solution.py:18
  284.8 7.5 %collective-permute-start.3 = (f32[4,1,128]{2,1,0:T(1,128)S(1)}, f32[4,1,128]{2,1,0:T(1,128)S(1)}, u32[]{:S(2)}, u32[]{:S(2)}) collective-permute-start(f32[4,1,128]{2,1,0:T(1,128)S(1)} %multiply_add_fusion.2), channel_id=1, source_target_pairs={{126,0},{0,2},{2,4},{4,6},{6,8},{8,10},{10,12},{12,14},{14,16},{16... | collective-permute-start | bytes 6152 | tf_op jit(solution)/shard_map/while/body/eval_jaxpr/ppermute | solution.py:18
  295.0 7.5 %collective-permute-start.3 = (f32[4,1,128]{2,1,0:T(1,128)S(1)}, f32[4,1,128]{2,1,0:T(1,128)S(1)}, u32[]{:S(2)}, u32[]{:S(2)}) collective-permute-start(f32[4,1,128]{2,1,0:T(1,128)S(1)} %multiply_add_fusion.2), channel_id=1, source_target_pairs={{126,0},{0,2},{2,4},{4,6},{6,8},{8,10},{10,12},{12,14},{14,16},{16... | collective-permute-start | bytes 6152 | tf_op jit(solution)/shard_map/while/body/eval_jaxpr/ppermute | solution.py:18
  305.3 7.5 %collective-permute-start.3 = (f32[4,1,128]{2,1,0:T(1,128)S(1)}, f32[4,1,128]{2,1,0:T(1,128)S(1)}, u32[]{:S(2)}, u32[]{:S(2)}) collective-permute-start(f32[4,1,128]{2,1,0:T(1,128)S(1)} %multiply_add_fusion.2), channel_id=1, source_target_pairs={{126,0},{0,2},{2,4},{4,6},{6,8},{8,10},{10,12},{12,14},{14,16},{16... | collective-permute-start | bytes 6152 | tf_op jit(solution)/shard_map/while/body/eval_jaxpr/ppermute | solution.py:18
  315.5 7.5 %collective-permute-start.3 = (f32[4,1,128]{2,1,0:T(1,128)S(1)}, f32[4,1,128]{2,1,0:T(1,128)S(1)}, u32[]{:S(2)}, u32[]{:S(2)}) collective-permute-start(f32[4,1,128]{2,1,0:T(1,128)S(1)} %multiply_add_fusion.2), channel_id=1, source_target_pairs={{126,0},{0,2},{2,4},{4,6},{6,8},{8,10},{10,12},{12,14},{14,16},{16... | collective-permute-start | bytes 6152 | tf_op jit(solution)/shard_map/while/body/eval_jaxpr/ppermute | solution.py:18
  325.7 7.5 %collective-permute-start.3 = (f32[4,1,128]{2,1,0:T(1,128)S(1)}, f32[4,1,128]{2,1,0:T(1,128)S(1)}, u32[]{:S(2)}, u32[]{:S(2)}) collective-permute-start(f32[4,1,128]{2,1,0:T(1,128)S(1)} %multiply_add_fusion.2), channel_id=1, source_target_pairs={{126,0},{0,2},{2,4},{4,6},{6,8},{8,10},{10,12},{12,14},{14,16},{16... | collective-permute-start | bytes 6152 | tf_op jit(solution)/shard_map/while/body/eval_jaxpr/ppermute | solution.py:18
  336.0 7.5 %collective-permute-start.3 = (f32[4,1,128]{2,1,0:T(1,128)S(1)}, f32[4,1,128]{2,1,0:T(1,128)S(1)}, u32[]{:S(2)}, u32[]{:S(2)}) collective-permute-start(f32[4,1,128]{2,1,0:T(1,128)S(1)} %multiply_add_fusion.2), channel_id=1, source_target_pairs={{126,0},{0,2},{2,4},{4,6},{6,8},{8,10},{10,12},{12,14},{14,16},{16... | collective-permute-start | bytes 6152 | tf_op jit(solution)/shard_map/while/body/eval_jaxpr/ppermute | solution.py:18
  346.2 7.5 %collective-permute-start.3 = (f32[4,1,128]{2,1,0:T(1,128)S(1)}, f32[4,1,128]{2,1,0:T(1,128)S(1)}, u32[]{:S(2)}, u32[]{:S(2)}) collective-permute-start(f32[4,1,128]{2,1,0:T(1,128)S(1)} %multiply_add_fusion.2), channel_id=1, source_target_pairs={{126,0},{0,2},{2,4},{4,6},{6,8},{8,10},{10,12},{12,14},{14,16},{16... | collective-permute-start | bytes 6152 | tf_op jit(solution)/shard_map/while/body/eval_jaxpr/ppermute | solution.py:18
  356.4 7.5 %collective-permute-start.3 = (f32[4,1,128]{2,1,0:T(1,128)S(1)}, f32[4,1,128]{2,1,0:T(1,128)S(1)}, u32[]{:S(2)}, u32[]{:S(2)}) collective-permute-start(f32[4,1,128]{2,1,0:T(1,128)S(1)} %multiply_add_fusion.2), channel_id=1, source_target_pairs={{126,0},{0,2},{2,4},{4,6},{6,8},{8,10},{10,12},{12,14},{14,16},{16... | collective-permute-start | bytes 6152 | tf_op jit(solution)/shard_map/while/body/eval_jaxpr/ppermute | solution.py:18
  366.7 7.5 %collective-permute-start.3 = (f32[4,1,128]{2,1,0:T(1,128)S(1)}, f32[4,1,128]{2,1,0:T(1,128)S(1)}, u32[]{:S(2)}, u32[]{:S(2)}) collective-permute-start(f32[4,1,128]{2,1,0:T(1,128)S(1)} %multiply_add_fusion.2), channel_id=1, source_target_pairs={{126,0},{0,2},{2,4},{4,6},{6,8},{8,10},{10,12},{12,14},{14,16},{16... | collective-permute-start | bytes 6152 | tf_op jit(solution)/shard_map/while/body/eval_jaxpr/ppermute | solution.py:18
  376.9 7.5 %collective-permute-start.3 = (f32[4,1,128]{2,1,0:T(1,128)S(1)}, f32[4,1,128]{2,1,0:T(1,128)S(1)}, u32[]{:S(2)}, u32[]{:S(2)}) collective-permute-start(f32[4,1,128]{2,1,0:T(1,128)S(1)} %multiply_add_fusion.2), channel_id=1, source_target_pairs={{126,0},{0,2},{2,4},{4,6},{6,8},{8,10},{10,12},{12,14},{14,16},{16... | collective-permute-start | bytes 6152 | tf_op jit(solution)/shard_map/while/body/eval_jaxpr/ppermute | solution.py:18
  387.2 7.5 %collective-permute-start.3 = (f32[4,1,128]{2,1,0:T(1,128)S(1)}, f32[4,1,128]{2,1,0:T(1,128)S(1)}, u32[]{:S(2)}, u32[]{:S(2)}) collective-permute-start(f32[4,1,128]{2,1,0:T(1,128)S(1)} %multiply_add_fusion.2), channel_id=1, source_target_pairs={{126,0},{0,2},{2,4},{4,6},{6,8},{8,10},{10,12},{12,14},{14,16},{16... | collective-permute-start | bytes 6152 | tf_op jit(solution)/shard_map/while/body/eval_jaxpr/ppermute | solution.py:18
  397.4 7.5 %collective-permute-start.3 = (f32[4,1,128]{2,1,0:T(1,128)S(1)}, f32[4,1,128]{2,1,0:T(1,128)S(1)}, u32[]{:S(2)}, u32[]{:S(2)}) collective-permute-start(f32[4,1,128]{2,1,0:T(1,128)S(1)} %multiply_add_fusion.2), channel_id=1, source_target_pairs={{126,0},{0,2},{2,4},{4,6},{6,8},{8,10},{10,12},{12,14},{14,16},{16... | collective-permute-start | bytes 6152 | tf_op jit(solution)/shard_map/while/body/eval_jaxpr/ppermute | solution.py:18
  407.6 7.5 %collective-permute-start.3 = (f32[4,1,128]{2,1,0:T(1,128)S(1)}, f32[4,1,128]{2,1,0:T(1,128)S(1)}, u32[]{:S(2)}, u32[]{:S(2)}) collective-permute-start(f32[4,1,128]{2,1,0:T(1,128)S(1)} %multiply_add_fusion.2), channel_id=1, source_target_pairs={{126,0},{0,2},{2,4},{4,6},{6,8},{8,10},{10,12},{12,14},{14,16},{16... | collective-permute-start | bytes 6152 | tf_op jit(solution)/shard_map/while/body/eval_jaxpr/ppermute | solution.py:18
  417.9 7.5 %collective-permute-start.3 = (f32[4,1,128]{2,1,0:T(1,128)S(1)}, f32[4,1,128]{2,1,0:T(1,128)S(1)}, u32[]{:S(2)}, u32[]{:S(2)}) collective-permute-start(f32[4,1,128]{2,1,0:T(1,128)S(1)} %multiply_add_fusion.2), channel_id=1, source_target_pairs={{126,0},{0,2},{2,4},{4,6},{6,8},{8,10},{10,12},{12,14},{14,16},{16... | collective-permute-start | bytes 6152 | tf_op jit(solution)/shard_map/while/body/eval_jaxpr/ppermute | solution.py:18
  428.1 7.5 %collective-permute-start.3 = (f32[4,1,128]{2,1,0:T(1,128)S(1)}, f32[4,1,128]{2,1,0:T(1,128)S(1)}, u32[]{:S(2)}, u32[]{:S(2)}) collective-permute-start(f32[4,1,128]{2,1,0:T(1,128)S(1)} %multiply_add_fusion.2), channel_id=1, source_target_pairs={{126,0},{0,2},{2,4},{4,6},{6,8},{8,10},{10,12},{12,14},{14,16},{16... | collective-permute-start | bytes 6152 | tf_op jit(solution)/shard_map/while/body/eval_jaxpr/ppermute | solution.py:18
  438.3 7.5 %collective-permute-start.3 = (f32[4,1,128]{2,1,0:T(1,128)S(1)}, f32[4,1,128]{2,1,0:T(1,128)S(1)}, u32[]{:S(2)}, u32[]{:S(2)}) collective-permute-start(f32[4,1,128]{2,1,0:T(1,128)S(1)} %multiply_add_fusion.2), channel_id=1, source_target_pairs={{126,0},{0,2},{2,4},{4,6},{6,8},{8,10},{10,12},{12,14},{14,16},{16... | collective-permute-start | bytes 6152 | tf_op jit(solution)/shard_map/while/body/eval_jaxpr/ppermute | solution.py:18
  448.6 7.5 %collective-permute-start.3 = (f32[4,1,128]{2,1,0:T(1,128)S(1)}, f32[4,1,128]{2,1,0:T(1,128)S(1)}, u32[]{:S(2)}, u32[]{:S(2)}) collective-permute-start(f32[4,1,128]{2,1,0:T(1,128)S(1)} %multiply_add_fusion.2), channel_id=1, source_target_pairs={{126,0},{0,2},{2,4},{4,6},{6,8},{8,10},{10,12},{12,14},{14,16},{16... | collective-permute-start | bytes 6152 | tf_op jit(solution)/shard_map/while/body/eval_jaxpr/ppermute | solution.py:18
  458.8 7.5 %collective-permute-start.3 = (f32[4,1,128]{2,1,0:T(1,128)S(1)}, f32[4,1,128]{2,1,0:T(1,128)S(1)}, u32[]{:S(2)}, u32[]{:S(2)}) collective-permute-start(f32[4,1,128]{2,1,0:T(1,128)S(1)} %multiply_add_fusion.2), channel_id=1, source_target_pairs={{126,0},{0,2},{2,4},{4,6},{6,8},{8,10},{10,12},{12,14},{14,16},{16... | collective-permute-start | bytes 6152 | tf_op jit(solution)/shard_map/while/body/eval_jaxpr/ppermute | solution.py:18
  469.0 7.5 %collective-permute-start.3 = (f32[4,1,128]{2,1,0:T(1,128)S(1)}, f32[4,1,128]{2,1,0:T(1,128)S(1)}, u32[]{:S(2)}, u32[]{:S(2)}) collective-permute-start(f32[4,1,128]{2,1,0:T(1,128)S(1)} %multiply_add_fusion.2), channel_id=1, source_target_pairs={{126,0},{0,2},{2,4},{4,6},{6,8},{8,10},{10,12},{12,14},{14,16},{16... | collective-permute-start | bytes 6152 | tf_op jit(solution)/shard_map/while/body/eval_jaxpr/ppermute | solution.py:18
  479.3 7.5 %collective-permute-start.3 = (f32[4,1,128]{2,1,0:T(1,128)S(1)}, f32[4,1,128]{2,1,0:T(1,128)S(1)}, u32[]{:S(2)}, u32[]{:S(2)}) collective-permute-start(f32[4,1,128]{2,1,0:T(1,128)S(1)} %multiply_add_fusion.2), channel_id=1, source_target_pairs={{126,0},{0,2},{2,4},{4,6},{6,8},{8,10},{10,12},{12,14},{14,16},{16... | collective-permute-start | bytes 6152 | tf_op jit(solution)/shard_map/while/body/eval_jaxpr/ppermute | solution.py:18
  489.5 7.5 %collective-permute-start.3 = (f32[4,1,128]{2,1,0:T(1,128)S(1)}, f32[4,1,128]{2,1,0:T(1,128)S(1)}, u32[]{:S(2)}, u32[]{:S(2)}) collective-permute-start(f32[4,1,128]{2,1,0:T(1,128)S(1)} %multiply_add_fusion.2), channel_id=1, source_target_pairs={{126,0},{0,2},{2,4},{4,6},{6,8},{8,10},{10,12},{12,14},{14,16},{16... | collective-permute-start | bytes 6152 | tf_op jit(solution)/shard_map/while/body/eval_jaxpr/ppermute | solution.py:18
  499.8 7.5 %collective-permute-start.3 = (f32[4,1,128]{2,1,0:T(1,128)S(1)}, f32[4,1,128]{2,1,0:T(1,128)S(1)}, u32[]{:S(2)}, u32[]{:S(2)}) collective-permute-start(f32[4,1,128]{2,1,0:T(1,128)S(1)} %multiply_add_fusion.2), channel_id=1, source_target_pairs={{126,0},{0,2},{2,4},{4,6},{6,8},{8,10},{10,12},{12,14},{14,16},{16... | collective-permute-start | bytes 6152 | tf_op jit(solution)/shard_map/while/body/eval_jaxpr/ppermute | solution.py:18
  561.2 7.5 %collective-permute-start.3 = (f32[4,1,128]{2,1,0:T(1,128)S(1)}, f32[4,1,128]{2,1,0:T(1,128)S(1)}, u32[]{:S(2)}, u32[]{:S(2)}) collective-permute-start(f32[4,1,128]{2,1,0:T(1,128)S(1)} %multiply_add_fusion.2), channel_id=1, source_target_pairs={{126,0},{0,2},{2,4},{4,6},{6,8},{8,10},{10,12},{12,14},{14,16},{16... | collective-permute-start | bytes 6152 | tf_op jit(solution)/shard_map/while/body/eval_jaxpr/ppermute | solution.py:18
  612.3 7.5 %collective-permute-start.3 = (f32[4,1,128]{2,1,0:T(1,128)S(1)}, f32[4,1,128]{2,1,0:T(1,128)S(1)}, u32[]{:S(2)}, u32[]{:S(2)}) collective-permute-start(f32[4,1,128]{2,1,0:T(1,128)S(1)} %multiply_add_fusion.2), channel_id=1, source_target_pairs={{126,0},{0,2},{2,4},{4,6},{6,8},{8,10},{10,12},{12,14},{14,16},{16... | collective-permute-start | bytes 6152 | tf_op jit(solution)/shard_map/while/body/eval_jaxpr/ppermute | solution.py:18
  (272 other events, 1626.7 us)
where the time goes:
time: 681 us; the launch traced here: 673 us
  waiting for transfers between devices  450 us (66%)
  matrix products  94.4 us (14%)
  local copies, waits for them, and re-layouts  55 us (8%)
  other arithmetic  42 us (6%)
  starting transfers between devices  27.2 us (4%)
    ppermute x256, waiting for transfers between devices, from_behind(): return lax.ppermute(block, axis, route)  450 us
    dot_general x64, matrix products, visit(): jnp.einsum('hrd,nhd->hrn', block, flat_keys, preferred_element_type=jnp.f...  58.2 us
    while x192, local copies, waits for them, and re-layouts  37.9 us
    dot_general x64, matrix products, visit(): jnp.einsum('hrn,nhd->hrd', weights.astype(jnp.bfloat16), flat_values, pre...  34.5 us
    ppermute x256, starting transfers between devices, from_behind(): return lax.ppermute(block, axis, route)  27.2 us
    convert_element_type x64, other arithmetic, visit(): weights.astype(jnp.bfloat16)  14 us
  transfers between devices with their start and end apart: 256, of which 128 were waited for; matrix products, arithmetic and copies ran while one was open for 0% of the time, Pallas kernels for 0%

commit v1 on v0

v1 whole, which is shorter than its diff:
```python
import functools

import jax
import jax.numpy as jnp
from jax import lax
from jax.experimental import pallas as pl
from jax.experimental.pallas import tpu as pltpu
from jax.sharding import PartitionSpec as P

QUERY_HEADS = 64
KEY_VALUE_HEADS = 8
HEAD_SIZE = 128
NEW_TOKENS = 2

LOG2E = 1.4426950408889634
MASKED = -1e30
FLOOR = -1e29
CODE = 512
SHARED = (((1,), (1,)), ((), ()))


def first_max(values):
    return functools.reduce(jnp.maximum, values)


def kernel(
    n,
    table_hbm,
    lengths_hbm,
    queries_hbm,
    keys_hbm,
    values_hbm,
    cache_hbm,
    out_ref,
    cache,
    table,
    lengths,
    own_query,
    fresh_keys,
    fresh_values,
    query,
    gathered,
    partial,
    received,
    local_sem,
    cache_sem,
    query_sems,
    partial_sems,
):
    me = lax.axis_index("ctx")
    slots, _, page, width = cache.shape
    kv_local = width // HEAD_SIZE
    seq_count, seq_pages = table.shape
    seq_rows = n // seq_count
    group = seq_rows // NEW_TOKENS
    factor = HEAD_SIZE ** (-0.5) * LOG2E

    small = [
        pltpu.make_async_copy(source, target, local_sem.at[i])
        for i, (source, target) in enumerate(
            (
                (queries_hbm, own_query),
                (table_hbm, table),
                (lengths_hbm, lengths),
                (keys_hbm, fresh_keys),
                (values_hbm, fresh_values),
            )
        )
    ]
    for copy in small:
        copy.start()
    pages = [
        pltpu.make_async_copy(cache_hbm.at[k], cache.at[k], cache_sem.at[k])
        for k in range(slots)
    ]
    for copy in pages:
        copy.start()

    barrier = pltpu.get_barrier_semaphore()

    def greet(j, carry):
        pl.semaphore_signal(barrier, inc=1, device_id={"ctx": lax.rem(me + j, n)})
        return carry

    lax.fori_loop(1, n, greet, 0)

    small[0].wait()
    for h in range(kv_local):
        query[pl.ds(h, 1), :] = own_query[h].astype(jnp.float32)
        gathered[me, pl.ds(h, 1), :] = own_query[h].astype(jnp.float32)
    pl.semaphore_wait(barrier, n - 1)

    def send_query(j, carry):
        pltpu.make_async_remote_copy(
            src_ref=query,
            dst_ref=gathered.at[me],
            send_sem=query_sems.at[0],
            recv_sem=query_sems.at[1],
            device_id={"ctx": lax.rem(me + j, n)},
        ).start()
        return carry

    lax.fori_loop(1, n, send_query, 0)

    for copy in small[1:]:
        copy.wait()

    of_seq = lax.broadcasted_iota(jnp.int32, (seq_count, seq_pages), 0)
    of_page = lax.broadcasted_iota(jnp.int32, (seq_count, seq_pages), 1)
    length = jnp.zeros((seq_count, seq_pages), jnp.int32)
    for s in range(seq_count):
        length = jnp.where(of_seq == s, lengths[s], length)
    held = jnp.clip(length - of_page * page, 0, page)
    code = (of_seq * CODE + held).astype(jnp.float32)
    entries = table[...]
    codes = [
        jnp.sum(
            jnp.where(entries == me * slots + k, code, 0.0), axis=(0, 1), keepdims=True
        )
        for k in range(slots)
    ]
    slot_seq = []
    slot_held = []
    for k in range(slots):
        seq = functools.reduce(
            jnp.add,
            [(codes[k] >= float(CODE * s)).astype(jnp.float32) for s in range(1, seq_count)],
        )
        slot_seq.append(seq)
        slot_held.append((codes[k] - float(CODE) * seq).astype(jnp.int32))

    row_seq = me // seq_rows
    row_step = lax.rem(me, seq_rows) // group
    token = lax.broadcasted_iota(jnp.int32, (seq_count * NEW_TOKENS, 1), 0)
    visible = (token // NEW_TOKENS == row_seq) & (lax.rem(token, NEW_TOKENS) <= row_step)
    fresh = []
    for h in range(kv_local):
        q = own_query[h].astype(jnp.float32)
        score = jnp.sum(q * fresh_keys[h].astype(jnp.float32), axis=1, keepdims=True)
        score = jnp.where(visible, score, MASKED)
        top = jnp.max(score, axis=0, keepdims=True)
        weight = jnp.where(visible, jnp.exp2((score - top) * factor), 0.0)
        total = jnp.sum(weight, axis=0, keepdims=True)
        rounded = weight.astype(jnp.bfloat16).astype(jnp.float32)
        mixed = jnp.sum(
            rounded * fresh_values[h].astype(jnp.float32), axis=0, keepdims=True
        )
        fresh.append((top * factor, total, mixed))

    for copy in pages:
        copy.wait()
    pltpu.make_async_copy(
        gathered.at[pl.ds(0, n - 1)], gathered.at[pl.ds(0, n - 1)], query_sems.at[1]
    ).wait()

    by_head = [gathered[:, h, :] for h in range(kv_local)]
    position = lax.broadcasted_iota(jnp.int32, (1, page), 1)
    blank = jnp.zeros((seq_rows, HEAD_SIZE), jnp.float32)
    tops, totals, mixes = [], [], []
    for k in range(slots):
        chosen = []
        for h in range(kv_local):
            rows = by_head[h][:seq_rows]
            for s in range(1, seq_count):
                rows = jnp.where(
                    slot_seq[k] == float(s),
                    by_head[h][s * seq_rows : (s + 1) * seq_rows],
                    rows,
                )
            chosen.append(rows)
        scores = []
        for h in range(0, kv_local, 2):
            left = jnp.concatenate(
                [
                    jnp.concatenate([chosen[h], blank], axis=1),
                    jnp.concatenate([blank, chosen[h + 1]], axis=1),
                ],
                axis=0,
            ).astype(jnp.bfloat16)
            keys = cache[k, 0, :, h * HEAD_SIZE : (h + 2) * HEAD_SIZE]
            scores.append(
                lax.dot_general(left, keys, SHARED, preferred_element_type=jnp.float32)
            )
        score = jnp.concatenate(scores, axis=0)
        score = jnp.where(position < slot_held[k], score, MASKED)
        top = jnp.maximum(jnp.max(score, axis=1, keepdims=True), FLOOR)
        weight = jnp.exp2((score - top) * factor)
        tops.append(top)
        totals.append(jnp.sum(weight, axis=1, keepdims=True))
        rounded = weight.astype(jnp.bfloat16)
        mixed = []
        for h in range(0, kv_local, 2):
            values = cache[k, 1, :, h * HEAD_SIZE : (h + 2) * HEAD_SIZE]
            both = jnp.dot(
                rounded[h * seq_rows : (h + 2) * seq_rows],
                values,
                preferred_element_type=jnp.float32,
            )
            mixed.append(both[:seq_rows, :HEAD_SIZE])
            mixed.append(both[seq_rows:, HEAD_SIZE:])
        mixes.append(jnp.concatenate(mixed, axis=0))

    for s in range(seq_count):
        inside = [slot_seq[k] == float(s) for k in range(slots)]
        top = first_max([jnp.where(inside[k], tops[k], FLOOR) for k in range(slots)])
        total = jnp.zeros_like(totals[0])
        mixed = jnp.zeros_like(mixes[0])
        for k in range(slots):
            share = jnp.where(inside[k], jnp.exp2((tops[k] - top) * factor), 0.0)
            total = total + share * totals[k]
            mixed = mixed + share * mixes[k]
        some = total > 0.0
        safe = jnp.where(some, total, 1.0)
        mixed = mixed / safe
        mass = jnp.where(some, top * factor + jnp.log2(safe), MASKED)
        mass = jnp.broadcast_to(mass, mixed.shape)
        rows = pl.ds(s * seq_rows, seq_rows)
        for h in range(kv_local):
            part = slice(h * seq_rows, (h + 1) * seq_rows)
            partial[rows, h, :] = mixed[part]
            partial[rows, kv_local + h, :] = mass[part]

    def send_partial(j, carry):
        peer = lax.rem(me + j, n)
        pltpu.make_async_remote_copy(
            src_ref=partial.at[peer],
            dst_ref=received.at[me],
            send_sem=partial_sems.at[0],
            recv_sem=partial_sems.at[1],
            device_id={"ctx": peer},
        ).start()
        return carry

    lax.fori_loop(1, n, send_partial, 0)
    received[me] = partial[me]

    pltpu.make_async_copy(
        received.at[pl.ds(0, n - 1)], received.at[pl.ds(0, n - 1)], partial_sems.at[1]
    ).wait()
    for h in range(kv_local):
        fresh_top, fresh_total, fresh_mixed = fresh[h]
        mixed = received[:, h, :]
        mass = received[:, kv_local + h, :]
        top = jnp.maximum(jnp.max(mass, axis=0, keepdims=True), fresh_top)
        share = jnp.exp2(mass - top)
        fresh_share = jnp.exp2(fresh_top - top)
        total = jnp.sum(share, axis=0, keepdims=True) + fresh_share * fresh_total
        sum_ = jnp.sum(share * mixed, axis=0, keepdims=True) + fresh_share * fresh_mixed
        out_ref[h] = (sum_ / total).astype(jnp.bfloat16)

    pltpu.make_async_copy(
        gathered.at[pl.ds(0, n - 1)], gathered.at[pl.ds(0, n - 1)], query_sems.at[0]
    ).wait()
    pltpu.make_async_copy(
        received.at[pl.ds(0, n - 1)], received.at[pl.ds(0, n - 1)], partial_sems.at[0]
    ).wait()


def solution(mesh):
    n = mesh.shape["ctx"]

    def on_device(queries, incoming_keys, incoming_values, paged_cache, page_table, lengths):
        kv_local = queries.shape[0]
        anywhere = pl.BlockSpec(memory_space=pl.ANY)
        return pl.pallas_call(
            functools.partial(kernel, n),
            out_shape=jax.ShapeDtypeStruct(queries.shape, queries.dtype),
            in_specs=[anywhere] * 6,
            out_specs=pl.BlockSpec(memory_space=pltpu.VMEM),
            scratch_shapes=[
                pltpu.VMEM(paged_cache.shape, paged_cache.dtype),
                pltpu.VMEM(page_table.shape, page_table.dtype),
                pltpu.SMEM(lengths.shape, lengths.dtype),
                pltpu.VMEM(queries.shape, queries.dtype),
                pltpu.VMEM(incoming_keys.shape, incoming_keys.dtype),
                pltpu.VMEM(incoming_values.shape, incoming_values.dtype),
                pltpu.VMEM((kv_local, HEAD_SIZE), jnp.float32),
                pltpu.VMEM((n, kv_local, HEAD_SIZE), jnp.float32),
                pltpu.VMEM((n, 2 * kv_local, HEAD_SIZE), jnp.float32),
                pltpu.VMEM((n, 2 * kv_local, HEAD_SIZE), jnp.float32),
                pltpu.SemaphoreType.DMA((5,)),
                pltpu.SemaphoreType.DMA((paged_cache.shape[0],)),
                pltpu.SemaphoreType.DMA((2,)),
                pltpu.SemaphoreType.DMA((2,)),
            ],
            compiler_params=pltpu.CompilerParams(collective_id=0, has_side_effects=True),
        )(page_table, lengths, queries, incoming_keys, incoming_values, paged_cache)

    in_specs = (
        P("head", "ctx", None),
        P("head", None, None),
        P("head", None, None),
        P("ctx", None, None, "head"),
        P(),
        P(),
    )
    return jax.shard_map(
        on_device,
        mesh=mesh,
        in_specs=in_specs,
        out_specs=P("head", "ctx", None),
        check_vma=False,
    )
```

time: 681 us -> 28.5 us (0.04); the launches traced: 673 us -> 28.3 us
  waiting for transfers between devices: 450 us -> 0 us
  matrix products: 94.4 us -> 0 us
  local copies, waits for them, and re-layouts: 55 us -> 2.51 us
  other arithmetic: 42 us -> 0 us
  starting transfers between devices: 27.2 us -> 0 us
  Pallas kernels: 0 us -> 25.8 us
    ppermute x256 -> x0, waiting for transfers between devices: 450 us -> none  [from_behind(): return lax.ppermute(block, axis, route)]
    dot_general x130 -> x0, matrix products: 94.4 us -> none  [the longest x64 58.2 us: visit(): jnp.einsum('hrd,nhd->hrn', block, flat_keys, preferred_element_type=jnp.f...]
    while x192 -> x0, local copies, waits for them, and re-layouts: 37.9 us -> none
    ppermute x256 -> x0, starting transfers between devices: 27.2 us -> none  [from_behind(): return lax.ppermute(block, axis, route)]
    pallas_call x0 -> x1, Pallas kernels: none -> 25.8 us  [on_device(): pl.pallas_call(functools.partial(kernel, n), out_shape=jax.ShapeDtypeStru...]
    convert_element_type x65 -> x0, other arithmetic: 14.6 us -> none  [the longest x64 14 us: visit(): weights.astype(jnp.bfloat16)]
    reduce_max x65 -> x0, other arithmetic: 9.89 us -> none  [the longest x64 9.8 us: visit(): top = jnp.max(scores, axis=-1)]
    another operation x4 -> x0, local copies, waits for them, and re-layouts: 9.29 us -> none  [the longest x1 5.53 us: on_device(): flat_values = page_values.reshape(slots * page, kv_local, HEAD_SIZE)]
  transfers between devices with their start and end apart: 256 -> 0, of which waited for: 128 -> 0; matrix products, arithmetic and copies ran while one was open for 0% -> 0% of each run, Pallas kernels for 0% -> 0%
where the time goes in v1:
time: 28.5 us; the launch traced here: 28.3 us
  Pallas kernels  25.8 us (91%)
  local copies, waits for them, and re-layouts  2.51 us (9%)
    pallas_call x1, Pallas kernels, on_device(): pl.pallas_call(functools.partial(kernel, n), out_shape=jax.ShapeDtypeStru...  25.8 us
    unnamed x1, local copies, waits for them, and re-layouts  1.27 us
    pallas_call x1, local copies, waits for them, and re-layouts, on_device(): pl.pallas_call(functools.partial(kernel, n), out_shape=jax.ShapeDtypeStru...  1.24 us

profile of v1, /device:TPU:1, one launch (start us, length us, event | category | flops | bytes accessed | tf_op | source)
XLA Modules:
  0.0 28.3 jit_solution(5487736483159566106)
XLA Ops:
  0.0 1.3 %copy.7.queries_hbm = bf16[4,1,128]{2,1,0:T(2,128)(2,1)} copy(bf16[4,1,128]{2,0,1:T(4,128)(2,1)} %param.6) | data formatting | bytes 2048 | tf_op args[0]
  1.3 25.8 %shard_map.64 = bf16[4,1,128]{2,1,0:T(2,128)(2,1)} custom-call(s32[4,192]{1,0:T(4,128)} %table_hbm.1, s32[4]{0:T(128)} %lengths_hbm.1, bf16[4,1,128]{2,1,0:T(2,128)(2,1)} %copy.7.queries_hbm, bf16[4,8,128]{2,1,0:T(8,128)(2,1)} %keys_hbm.1, bf16[4,8,128]{2,1,0:T(8,128)(2,1)} %values_hbm.1, bf16[12,2,256,512]{3,2,1,0:T(8,128)(2,1)} %cache_hbm.1), custom_call_target="tpu_custom_call" | custom-call | tf_op jit(solution)/shard_map/pallas_call | solution.py:265
  27.1 1.2 %copy.8 = bf16[4,1,128]{2,0,1:T(4,128)(2,1)} copy(bf16[4,1,128]{2,1,0:T(2,128)(2,1)} %shard_map.64) | data formatting | bytes 2048 | tf_op jit(solution)/shard_map/pallas_call | solution.py:265

commit v2 on v1

v2 whole, which is shorter than its diff:
```python
import functools

import jax
import jax.numpy as jnp
from jax import lax
from jax.experimental import pallas as pl
from jax.experimental.pallas import tpu as pltpu
from jax.sharding import PartitionSpec as P

QUERY_HEADS = 64
KEY_VALUE_HEADS = 8
HEAD_SIZE = 128
NEW_TOKENS = 2

LOG2E = 1.4426950408889634
MASKED = -1e30
FLOOR = -1e29
CODE = 512
SUBLANES = 8
SHARED = (((1,), (1,)), ((), ()))


def kernel(
    n,
    table_hbm,
    lengths_hbm,
    queries_hbm,
    keys_hbm,
    values_hbm,
    cache_hbm,
    out_ref,
    cache,
    table,
    lengths,
    own_query,
    fresh_keys,
    fresh_values,
    query,
    gathered,
    marks,
    bias,
    wide,
    partial,
    received,
    local_sem,
    cache_sem,
    query_sems,
    partial_sems,
):
    me = lax.axis_index("ctx")
    slots, _, page, width = cache.shape
    kv_local = width // HEAD_SIZE
    seq_count, seq_pages = table.shape
    seq_rows = n // seq_count
    group = seq_rows // NEW_TOKENS
    factor = HEAD_SIZE ** (-0.5) * LOG2E
    tiles = kv_local * seq_rows // SUBLANES

    my_seq = me // seq_rows
    my_place = lax.rem(me, seq_rows)
    seq_at = [lax.rem(my_seq + d, seq_count) for d in range(seq_count)]
    place_at = [lax.rem(my_place + d, seq_rows) for d in range(seq_rows)]
    seq_order = sorted(range(seq_count), key=lambda d: -min(d, seq_count - d))
    place_order = sorted(range(seq_rows), key=lambda d: -min(d, seq_rows - d))
    others = [(d, e) for d in seq_order for e in place_order if d or e]

    def peer(d, e):
        return seq_at[d] * seq_rows + place_at[e]

    small = [
        pltpu.make_async_copy(source, target, local_sem.at[i])
        for i, (source, target) in enumerate(
            (
                (queries_hbm, own_query),
                (table_hbm, table),
                (lengths_hbm, lengths),
                (keys_hbm, fresh_keys),
                (values_hbm, fresh_values),
            )
        )
    ]
    small[0].start()
    barrier = pltpu.get_barrier_semaphore()
    for d, e in others:
        pl.semaphore_signal(barrier, inc=1, device_id={"ctx": peer(d, e)})
    for copy in small[1:]:
        copy.start()
    pages = [
        pltpu.make_async_copy(cache_hbm.at[k], cache.at[k], cache_sem.at[k])
        for k in range(slots)
    ]
    for copy in pages:
        copy.start()

    small[0].wait()
    for h in range(kv_local):
        row = own_query[pl.ds(h, 1), :].astype(jnp.float32)
        query[pl.ds(h, 1), :] = row
        gathered[me, pl.ds(h, 1), :] = row
    pl.semaphore_wait(barrier, n - 1)

    for d, e in others:
        pltpu.make_async_remote_copy(
            src_ref=query,
            dst_ref=gathered.at[me],
            send_sem=query_sems.at[0],
            recv_sem=query_sems.at[1],
            device_id={"ctx": peer(d, e)},
        ).start()

    for copy in small[1:]:
        copy.wait()

    of_seq = lax.broadcasted_iota(jnp.int32, (seq_count, seq_pages), 0)
    of_page = lax.broadcasted_iota(jnp.int32, (seq_count, seq_pages), 1)
    length = jnp.zeros((seq_count, seq_pages), jnp.int32)
    for s in range(seq_count):
        length = jnp.where(of_seq == s, lengths[s], length)
    held = jnp.clip(length - of_page * page, 0, page)
    code = (of_seq * CODE + held).astype(jnp.float32)
    entries = table[...]
    position = lax.broadcasted_iota(jnp.int32, (SUBLANES, page), 1).astype(jnp.float32)
    for k in range(slots):
        found = jnp.where(entries == me * slots + k, code, 0.0)
        found = jnp.sum(found, axis=(0, 1), keepdims=True)
        found = jnp.broadcast_to(found, (SUBLANES, HEAD_SIZE))
        count = found
        for s in range(seq_count):
            inside = (found >= float(CODE * s)) & (found < float(CODE * (s + 1)))
            marks[k, s] = jnp.where(inside, 1.0, 0.0)
            count = jnp.where(inside, found - float(CODE * s), count)
        count = jnp.concatenate([count] * (page // HEAD_SIZE), axis=1)
        bias[k] = jnp.where(position < count, 0.0, MASKED)

    row_step = my_place // group
    token = lax.broadcasted_iota(jnp.int32, (seq_count * NEW_TOKENS, 1), 0)
    visible = (token // NEW_TOKENS == my_seq) & (lax.rem(token, NEW_TOKENS) <= row_step)
    fresh = []
    for h in range(kv_local):
        q = own_query[pl.ds(h, 1), :].astype(jnp.float32)
        score = jnp.sum(q * fresh_keys[h].astype(jnp.float32), axis=1, keepdims=True)
        score = jnp.where(visible, score, MASKED)
        top = jnp.max(score, axis=0, keepdims=True)
        weight = jnp.where(visible, jnp.exp2((score - top) * factor), 0.0)
        total = jnp.sum(weight, axis=0, keepdims=True)
        rounded = weight.astype(jnp.bfloat16).astype(jnp.float32)
        mixed = jnp.sum(
            rounded * fresh_values[h].astype(jnp.float32), axis=0, keepdims=True
        )
        fresh.append((top * factor, total, mixed))

    for copy in pages:
        copy.wait()
    arrived = gathered.at[pl.ds(0, n - 1)]
    pltpu.make_async_copy(arrived, arrived, query_sems.at[1]).wait()

    by_head = [
        gathered[:, h, :].reshape(n // SUBLANES, SUBLANES, HEAD_SIZE) for h in range(kv_local)
    ]
    seq_tiles = seq_rows // SUBLANES
    blank = jnp.zeros((seq_rows, HEAD_SIZE), jnp.float32)

    def pick(k, choices):
        chosen = choices[0]
        for s in range(1, seq_count):
            chosen = jnp.where(marks[k, s][None] > 0.5, choices[s], chosen)
        return chosen

    scores = []
    tops = [jnp.full((tiles, SUBLANES, HEAD_SIZE), FLOOR, jnp.float32)] * seq_count
    for k in range(slots):
        chosen = [
            pick(
                k, [by_head[h][s * seq_tiles : (s + 1) * seq_tiles] for s in range(seq_count)]
            ).reshape(seq_rows, HEAD_SIZE)
            for h in range(kv_local)
        ]
        score = []
        for h in range(0, kv_local, 2):
            left = jnp.concatenate(
                [
                    jnp.concatenate([chosen[h], blank], axis=1),
                    jnp.concatenate([blank, chosen[h + 1]], axis=1),
                ],
                axis=0,
            ).astype(jnp.bfloat16)
            keys = cache[k, 0, :, h * HEAD_SIZE : (h + 2) * HEAD_SIZE]
            score.append(
                lax.dot_general(left, keys, SHARED, preferred_element_type=jnp.float32)
            )
        score = jnp.concatenate(score, axis=0).reshape(tiles, SUBLANES, page)
        score = score + bias[k][None]
        scores.append(score)
        top = functools.reduce(
            jnp.maximum,
            [score[:, :, i : i + HEAD_SIZE] for i in range(0, page, HEAD_SIZE)],
        )
        for s in range(seq_count):
            tops[s] = jnp.maximum(
                tops[s], jnp.where(marks[k, s][None] > 0.5, top, FLOOR)
            )
    tops = [
        jnp.broadcast_to(jnp.max(top, axis=2, keepdims=True), top.shape) for top in tops
    ]

    sums, mixes = [], []
    for k in range(slots):
        top = pick(k, tops)
        top = jnp.concatenate([top] * (page // HEAD_SIZE), axis=2)
        weight = jnp.exp2((scores[k] - top) * factor)
        sums.append(
            functools.reduce(
                jnp.add,
                [weight[:, :, i : i + HEAD_SIZE] for i in range(0, page, HEAD_SIZE)],
            )
        )
        rounded = weight.reshape(kv_local * seq_rows, page).astype(jnp.bfloat16)
        mixed = []
        for h in range(0, kv_local, 2):
            values = cache[k, 1, :, h * HEAD_SIZE : (h + 2) * HEAD_SIZE]
            both = jnp.dot(
                rounded[h * seq_rows : (h + 2) * seq_rows],
                values,
                preferred_element_type=jnp.float32,
            )
            mixed.append(both[:seq_rows, :HEAD_SIZE])
            mixed.append(both[seq_rows:, HEAD_SIZE:])
        mixes.append(
            jnp.concatenate(mixed, axis=0).reshape(tiles, SUBLANES, HEAD_SIZE)
        )

    lane = lax.broadcasted_iota(jnp.int32, (1, 1, HEAD_SIZE), 2)
    for s in range(seq_count):
        total = jnp.zeros_like(sums[0])
        mixed = jnp.zeros_like(mixes[0])
        for k in range(slots):
            mark = marks[k, s][None]
            total = total + mark * sums[k]
            mixed = mixed + mark * mixes[k]
        total = jnp.sum(total, axis=2, keepdims=True)
        some = total > 0.0
        safe = jnp.where(some, total, 1.0)
        mixed = mixed / safe
        mass = jnp.where(some, tops[s] * factor + jnp.log2(safe), MASKED)
        high = mass.astype(jnp.bfloat16).astype(jnp.float32)
        rest = mass - high
        middle = rest.astype(jnp.bfloat16).astype(jnp.float32)
        low = rest - middle
        mass = jnp.where(
            lane == 0, high, jnp.where(lane == 1, middle, jnp.where(lane == 2, low, 0.0))
        )
        mixed = mixed.reshape(kv_local * seq_rows, HEAD_SIZE)
        mass = mass.reshape(kv_local * seq_rows, HEAD_SIZE)
        rows = pl.ds(s * seq_rows, seq_rows)
        for h in range(kv_local):
            part = slice(h * seq_rows, (h + 1) * seq_rows)
            wide[rows, h, :] = mixed[part]
            wide[rows, kv_local + h, :] = mass[part]
        partial[rows] = wide[rows].astype(jnp.bfloat16)

    for d, e in others:
        partner = peer(d, e)
        pltpu.make_async_remote_copy(
            src_ref=partial.at[partner],
            dst_ref=received.at[me],
            send_sem=partial_sems.at[0],
            recv_sem=partial_sems.at[1],
            device_id={"ctx": partner},
        ).start()
    received[me] = partial[me]

    arrived = received.at[pl.ds(0, n - 1)]
    pltpu.make_async_copy(arrived, arrived, partial_sems.at[1]).wait()
    wide[...] = received[...].astype(jnp.float32)
    for h in range(kv_local):
        fresh_top, fresh_total, fresh_mixed = fresh[h]
        mixed = wide[:, h, :]
        mass = jnp.sum(wide[:, kv_local + h, :], axis=1, keepdims=True)
        top = jnp.maximum(jnp.max(mass, axis=0, keepdims=True), fresh_top)
        share = jnp.exp2(mass - top)
        fresh_share = jnp.exp2(fresh_top - top)
        total = jnp.sum(share, axis=0, keepdims=True) + fresh_share * fresh_total
        whole = jnp.sum(share * mixed, axis=0, keepdims=True) + fresh_share * fresh_mixed
        out_ref[pl.ds(h, 1), :] = (whole / total).astype(jnp.bfloat16)

    sent = gathered.at[pl.ds(0, n - 1)]
    pltpu.make_async_copy(sent, sent, query_sems.at[0]).wait()
    sent = received.at[pl.ds(0, n - 1)]
    pltpu.make_async_copy(sent, sent, partial_sems.at[0]).wait()


def solution(mesh):
    n = mesh.shape["ctx"]

    def on_device(queries, incoming_keys, incoming_values, paged_cache, page_table, lengths):
        kv_local = queries.shape[0]
        slots, _, page, _ = paged_cache.shape
        row = queries.reshape(kv_local, HEAD_SIZE)
        anywhere = pl.BlockSpec(memory_space=pl.ANY)
        attended = pl.pallas_call(
            functools.partial(kernel, n),
            out_shape=jax.ShapeDtypeStruct(row.shape, row.dtype),
            in_specs=[anywhere] * 6,
            out_specs=pl.BlockSpec(memory_space=pltpu.VMEM),
            scratch_shapes=[
                pltpu.VMEM(paged_cache.shape, paged_cache.dtype),
                pltpu.VMEM(page_table.shape, page_table.dtype),
                pltpu.SMEM(lengths.shape, lengths.dtype),
                pltpu.VMEM(row.shape, row.dtype),
                pltpu.VMEM(incoming_keys.shape, incoming_keys.dtype),
                pltpu.VMEM(incoming_values.shape, incoming_values.dtype),
                pltpu.VMEM((kv_local, HEAD_SIZE), jnp.float32),
                pltpu.VMEM((n, kv_local, HEAD_SIZE), jnp.float32),
                pltpu.VMEM((slots, page_table.shape[0], SUBLANES, HEAD_SIZE), jnp.float32),
                pltpu.VMEM((slots, SUBLANES, page), jnp.float32),
                pltpu.VMEM((n, 2 * kv_local, HEAD_SIZE), jnp.float32),
                pltpu.VMEM((n, 2 * kv_local, HEAD_SIZE), jnp.bfloat16),
                pltpu.VMEM((n, 2 * kv_local, HEAD_SIZE), jnp.bfloat16),
                pltpu.SemaphoreType.DMA((5,)),
                pltpu.SemaphoreType.DMA((slots,)),
                pltpu.SemaphoreType.DMA((2,)),
                pltpu.SemaphoreType.DMA((2,)),
            ],
            compiler_params=pltpu.CompilerParams(collective_id=0, has_side_effects=True),
        )(page_table, lengths, row, incoming_keys, incoming_values, paged_cache)
        return attended.reshape(queries.shape)

    in_specs = (
        P("head", "ctx", None),
        P("head", None, None),
        P("head", None, None),
        P("ctx", None, None, "head"),
        P(),
        P(),
    )
    return jax.shard_map(
        on_device,
        mesh=mesh,
        in_specs=in_specs,
        out_specs=P("head", "ctx", None),
        check_vma=False,
    )
```

time: 28.5 us -> 23.3 us (0.82)
  Pallas kernels: 25.8 us -> 21.9 us
  local copies, waits for them, and re-layouts: 2.51 us -> 1.24 us
    pallas_call x1, Pallas kernels: 25.8 us -> 21.9 us  [on_device(): pl.pallas_call(functools.partial(kernel, n), out_shape=jax.ShapeDtypeStru...]
    pallas_call x1 -> x0, local copies, waits for them, and re-layouts: 1.24 us -> none  [on_device(): pl.pallas_call(functools.partial(kernel, n), out_shape=jax.ShapeDtypeStru...]
where the time goes in v2:
time: 23.3 us; the launch traced here: 23.1 us
  Pallas kernels  21.9 us (94%)
  local copies, waits for them, and re-layouts  1.24 us (5%)
    pallas_call x1, Pallas kernels, on_device(): pl.pallas_call(functools.partial(kernel, n), out_shape=jax.ShapeDtypeStru...  21.9 us
    unnamed x1, local copies, waits for them, and re-layouts  1.24 us

profile of v2, /device:TPU:1, one launch (start us, length us, event | category | flops | bytes accessed | tf_op | source)
XLA Modules:
  0.0 23.1 jit_solution(12444684080975175075)
XLA Ops:
  0.0 21.9 %shard_map.64 = bf16[4,128]{1,0:T(4,128)(2,1)} custom-call(s32[4,192]{1,0:T(4,128)} %table_hbm.1, s32[4]{0:T(128)} %lengths_hbm.1, bf16[4,128]{1,0:T(4,128)(2,1)} %bitcast.3, bf16[4,8,128]{2,1,0:T(8,128)(2,1)} %keys_hbm.1, bf16[4,8,128]{2,1,0:T(8,128)(2,1)} %values_hbm.1, bf16[12,2,256,512]{3,2,1,0:T(8,128)(2,1)} %cache_hbm.1), custom_call_target="tpu_custom_call" | custom-call | tf_op jit(solution)/shard_map/pallas_call | solution.py:300
  21.9 1.2 %copy.8 = bf16[4,1,128]{2,0,1:T(4,128)(2,1)} copy(bf16[4,1,128]{2,0,1:T(4,128)(2,1)} %bitcast.2) | data formatting | bytes 2048

commit v3 on v2

--- a/solution.py
+++ b/solution.py
@@ -299,7 +299,7 @@
         anywhere = pl.BlockSpec(memory_space=pl.ANY)
         attended = pl.pallas_call(
             functools.partial(kernel, n),
-            out_shape=jax.ShapeDtypeStruct(row.shape, row.dtype),
+            out_shape=pltpu.VMEM(row.shape, row.dtype),
             in_specs=[anywhere] * 6,
             out_specs=pl.BlockSpec(memory_space=pltpu.VMEM),
             scratch_shapes=[

time: 23.3 us -> 22 us (0.944)
  local copies, waits for them, and re-layouts: 1.24 us -> 0.56 us
  Pallas kernels: 21.9 us -> 21.3 us
    unnamed x1, local copies, waits for them, and re-layouts: 1.24 us -> 0.56 us
    pallas_call x1, Pallas kernels: 21.9 us -> 21.3 us  [on_device(): pl.pallas_call(functools.partial(kernel, n), out_shape=pltpu.VMEM(row.sha...]
where the time goes in v3:
time: 22 us; the launch traced here: 21.9 us
  Pallas kernels  21.3 us (97%)
  local copies, waits for them, and re-layouts  0.56 us (3%)
    pallas_call x1, Pallas kernels, on_device(): pl.pallas_call(functools.partial(kernel, n), out_shape=pltpu.VMEM(row.sha...  21.3 us
    unnamed x1, local copies, waits for them, and re-layouts  0.56 us

profile of v3, /device:TPU:1, one launch (start us, length us, event | category | flops | bytes accessed | tf_op | source)
XLA Modules:
  0.0 21.9 jit_solution(16875170355487140649)
XLA Ops:
  0.0 21.3 %shard_map.64 = bf16[4,128]{1,0:T(4,128)(2,1)S(1)} custom-call(s32[4,192]{1,0:T(4,128)} %table_hbm.1, s32[4]{0:T(128)} %lengths_hbm.1, bf16[4,128]{1,0:T(4,128)(2,1)} %bitcast.3, bf16[4,8,128]{2,1,0:T(8,128)(2,1)} %keys_hbm.1, bf16[4,8,128]{2,1,0:T(8,128)(2,1)} %values_hbm.1, bf16[12,2,256,512]{3,2,1,0:T(8,128)(2,1)} %cache_hbm.1), custom_call_target="tpu_custom_call" | custom-call | tf_op jit(solution)/shard_map/pallas_call | solution.py:300
  21.3 0.6 %copy.8 = bf16[4,1,128]{2,0,1:T(4,128)(2,1)} copy(bf16[4,1,128]{2,0,1:T(4,128)(2,1)S(1)} %bitcast.2) | data formatting | bytes 2048
